TPU v7x, 32 devices: a whole 2x2x4 slice. The times are simulated.
32 devices in a mesh: grp: 1, wide: 8 (over z, y), narrow: 4 (over x, core).
Axes of the slice: x: 2, y: 2, z: 4, core: 2. Of those that a mesh axis runs over, the one named last changes fastest.
Arguments:
- vectors: bfloat16 [512, 2, 3, 16, 512], P('grp', None, None, 'wide', 'narrow'), may hold values from -6 to 6
- links: float32 [3, 2, 3, 3, 16, 512], P('grp', None, None, None, 'wide', 'narrow'), may hold values from -4 to 4
- directions: int32 [3], replicated, may hold values from 0 to 2, each once
- peram: bfloat16 [2, 512, 256], P('grp', 'wide', 'narrow'), may hold values from -0.1875 to 0.1875
Outputs:
- elementals: float32 [3, 2, 512, 512], P('grp', None, 'wide')
- products: float32 [3, 2, 512, 256], P('grp', None, 'wide', 'narrow')
All inputs are finite; a program needn't handle non-finite values.
Results may differ from a plain program's by a relative error of at most 0.004.
Values may be sent and summed in bfloat16 or wider, within the bound.
A program may use at most 64 MiB of HBM per device.

v0:
```python
import math

import jax
import jax.numpy as jnp
from jax import lax
from jax.sharding import PartitionSpec as P

LZ = 16


def from_behind(x, axis, by):
    length = lax.axis_size(axis)
    return lax.ppermute(x, axis, [(i, (i + by) % length) for i in range(length)])


def covariant_product(link_field, shifted):
    link_real = link_field[0][None]
    link_imag = link_field[1][None]
    vec_real = shifted[:, 0][:, None]
    vec_imag = shifted[:, 1][:, None]
    out_real = jnp.sum(link_real * vec_real - link_imag * vec_imag, axis=2)
    out_imag = jnp.sum(link_real * vec_imag + link_imag * vec_real, axis=2)
    return jnp.stack([out_real, out_imag], 1).astype(jnp.bfloat16)


def on_device(vectors, links, directions, peram):
    vec_count = vectors.shape[0]
    plane_count = vectors.shape[3]
    row_length = vectors.shape[4]
    direction_count = directions.shape[0]
    col_count = peram.shape[2]
    wide_count = lax.axis_size("wide")
    narrow_count = lax.axis_size("narrow")
    norm_factor = 1.0 / math.sqrt(12.0 * plane_count * wide_count * row_length * narrow_count)
    next_first = from_behind(vectors[:, :, :, 0:1], "wide", -1)
    along_first = jnp.concatenate([vectors[:, :, :, 1:], next_first], 3)
    next_second = from_behind(vectors[:, :, :, :, 0:LZ], "narrow", -1)
    along_second = jnp.concatenate([vectors[:, :, :, :, LZ:], next_second], 4)
    along_third = jnp.roll(
        vectors.reshape(vec_count, 2, 3, plane_count, row_length // LZ, LZ), -1, axis=5
    ).reshape(vectors.shape)
    rotated = jnp.concatenate([-vectors[:, 1:2], vectors[:, 0:1]], 1)
    left_block = jnp.concatenate(
        [vectors.reshape(vec_count, -1), rotated.reshape(vec_count, -1)], 0
    )
    partials = []
    for slot_index in range(direction_count):
        chosen = directions[slot_index]
        shifted = jnp.where(
            chosen == 0, along_first, jnp.where(chosen == 1, along_second, along_third)
        )
        link_field = jnp.where(chosen == 0, links[0], jnp.where(chosen == 1, links[1], links[2]))
        product = covariant_product(link_field, shifted).reshape(vec_count, -1)
        partials.append(
            lax.dot_general(
                left_block, product, (((1,), (1,)), ((), ())), preferred_element_type=jnp.float32
            )
        )
    halves = jnp.stack(partials).reshape(direction_count, 2, vec_count, vec_count) * norm_factor
    real_part = halves[:, 0]
    imag_part = halves[:, 1]
    local_terms = jnp.stack(
        [real_part - jnp.swapaxes(real_part, 1, 2), imag_part + jnp.swapaxes(imag_part, 1, 2)], 1
    )
    rows_here = vec_count // wide_count
    thin_rows = lax.psum_scatter(local_terms, ("wide", "narrow"), scatter_dimension=2, tiled=True)
    elementals = lax.all_gather(thin_rows, "narrow", axis=2, tiled=True)
    elem_low = elementals.astype(jnp.bfloat16)
    real_rows = elem_low[:, 0]
    imag_rows = elem_low[:, 1]
    piece = lax.all_gather(peram, "wide", axis=1, tiled=True)
    width = piece.shape[1]
    left_part = jnp.concatenate([real_rows, imag_rows], 2).reshape(-1, 2 * width)
    right_part = jnp.concatenate(
        [jnp.concatenate([piece[0], piece[1]], 1), jnp.concatenate([-piece[1], piece[0]], 1)], 0
    )
    summed = jnp.dot(left_part, right_part, preferred_element_type=jnp.float32)
    products = summed.reshape(direction_count, rows_here, 2, col_count).transpose(0, 2, 1, 3)
    return (elementals, products)


def solution(mesh):
    placed = (
        P("grp", None, None, "wide", "narrow"),
        P("grp", None, None, None, "wide", "narrow"),
        P(),
        P("grp", "wide", "narrow"),
    )
    return jax.shard_map(
        on_device,
        mesh=mesh,
        in_specs=placed,
        out_specs=(P("grp", None, "wide", None), P("grp", None, "wide", "narrow")),
        check_vma=False,
    )
```

profile of v0, /device:TPU:0, one launch (start us, length us, event | category | flops | bytes accessed | tf_op | source)
XLA Modules:
  0.0 246.1 jit_solution(10593543814689281994)
XLA Ops:
  7.2 3.6 %copy.27 = bf16[512,2,3,2,128]{0,4,3,2,1:T(8,128)(2,1)S(1)} copy(bf16[512,2,3,2,128]{4,3,2,1,0:T(2,128)(2,1)} %param.4) | data formatting | bytes 3145728 | tf_op args[0]
  12.1 6.0 %collective-permute-start = (bf16[512,2,3,1,128]{0,4,3,2,1:T(8,128)(2,1)}, bf16[512,2,3,1,128]{0,4,3,2,1:T(8,128)(2,1)}, u32[]{:S(2)}, u32[]{:S(2)}) collective-permute-start(bf16[512,2,3,1,128]{0,4,3,2,1:T(8,128)(2,1)} %get-tuple-element.28), channel_id=1, source_target_pairs={{0,28},{4,0},{8,4},{12,8},{16,12},{20,16},{24,20},{28,24},{1,29},{... | collective-permute-start | bytes 2359304 | tf_op jit(solution)/shard_map/ppermute | solution.py:13
  25.2 3.2 %pad_maximum_fusion.2 = bf16[512,2,3,2,128]{4,3,2,1,0:T(2,128)(2,1)} fusion(bf16[512,1,3,2,128]{4,3,2,1,0:T(2,128)(2,1)S(1)} %get-tuple-element.30, bf16[512,1,3,2,128]{4,3,2,1,0:T(2,128)(2,1)S(1)} %get-tuple-element.29), kind=kLoop, calls=%fused_computation.17 | loop fusion | flops 786432 | bytes 3145728 | tf_op jit(solution)/shard_map/concatenate | solution.py:42
  29.0 1.7 pad_maximum_fusion.5
  31.9 1.5 reshape.106
  36.6 3.4 %pad_maximum_fusion.1 = bf16[1024,1536]{1,0:T(8,128)(2,1)} fusion(bf16[512,1536]{1,0:T(8,128)(2,1)} %reshape.107, bf16[512,1536]{1,0:T(8,128)(2,1)S(1)} %copy-done.3), kind=kLoop, calls=%fused_computation.9 | loop fusion | flops 6291456 | bytes 6291456 | tf_op jit(solution)/shard_map/concatenate | solution.py:43
  40.7 3.5 %fusion.2 = (bf16[512,2,3,2,128]{0,4,3,2,1:T(8,128)(2,1)S(1)}, bf16[512,2,3,2,128]{0,4,3,2,1:T(8,128)(2,1)}, bf16[512,2,3,2,128]{0,4,3,2,1:T(8,128)(2,1)}) fusion(bf16[512,2,3,2,8,16]{0,5,4,3,2,1:T(8,128)(2,1)S(1)} %copy-done.5, pred[]{:T(512)} %bitcast.2, pred[]{:T(512)} %bitcast.1, bf16[512,2,3,2,16]{0,4,3,2,1:T(8,128)(2,1)S(1)} %collective-permute-done.1, ...), kind=kLoop, calls=%fused_computation.27 | loop fusion | flops 11010048 | bytes 9437190 | tf_op jit(solution)/shard_map/jit(_where)/select_n | solution.py:49
  44.2 1.6 fusion.10
  46.3 1.9 copy.33
  49.8 1.6 copy.34
  51.4 1.5 reshape.117
  52.9 4.4 %fusion.6 = (f32[512,3,2,128]{0,3,2,1:T(8,128)S(1)}, f32[512,3,2,128]{0,3,2,1:T(8,128)S(1)}, f32[512,3,2,128]{0,3,2,1:T(8,128)}, f32[512,3,2,128]{0,3,2,1:T(8,128)}) fusion(bf16[512,2,3,2,128]{0,4,3,2,1:T(8,128)(2,1)} %get-tuple-element.20, bf16[512,2,3,2,128]{0,4,3,2,1:T(8,128)(2,1)} %get-tuple-element.19), kind=kLoop, calls=%fused_computation.34 | loop fusion | flops 1572864 | bytes 9437184 | tf_op jit(solution)/shard_map/mul | solution.py:21
  57.4 3.1 %copy.35 = f32[512,3,2,128]{3,0,2,1:T(8,128)} copy(f32[512,3,2,128]{0,3,2,1:T(8,128)} %get-tuple-element.48) | data formatting | bytes 3145728 | tf_op jit(solution)/shard_map/mul | solution.py:21
  60.5 3.1 %copy.36 = f32[512,3,2,128]{3,0,2,1:T(8,128)} copy(f32[512,3,2,128]{0,3,2,1:T(8,128)} %get-tuple-element.47) | data formatting | bytes 3145728 | tf_op jit(solution)/shard_map/mul | solution.py:21
  63.6 3.3 %subtract_reduce_fusion.1 = (bf16[512,3,2,128]{3,0,2,1:T(8,128)(2,1)S(1)}, bf16[512,3,2,128]{3,0,2,1:T(8,128)(2,1)S(1)}) fusion(f32[512,3,2,128]{3,0,2,1:T(8,128)} %copy.36, f32[3,3,2,128]{3,2,1,0:T(2,128)S(1)} %copy-done.15, f32[512,3,2,128]{3,0,2,1:T(8,128)} %copy.35, f32[3,3,2,128]{3,2,1,0:T(2,128)S(1)} %copy-done.16), kind=kLoop, calls=%fused_computation.5 | loop fusion | flops 8650752 | bytes 4737024 | tf_op jit(solution)/shard_map/reduce_sum | solution.py:21
  67.0 2.8 %copy.37 = bf16[512,2,3,2,128]{4,3,2,1,0:T(2,128)(2,1)} copy(bf16[512,2,3,2,128]{4,0,3,2,1:T(8,128)(2,1)S(1)} %pad_maximum_fusion.7) | data formatting | bytes 3145728 | tf_op jit(solution)/shard_map/stack | solution.py:23
  69.8 4.9 %reshape.118 = bf16[512,1536,1]{1,0,2:T(8,128)(2,1)} reshape(bf16[512,2,3,2,128]{4,3,2,1,0:T(2,128)(2,1)} %copy.37) | data formatting | bytes 3145728 | tf_op jit(solution)/shard_map/convert_element_type | solution.py:23
  74.7 5.7 %convolution_bitcast_fusion.2 = f32[1,2,512,512]{3,2,1,0:T(8,128)} fusion(bf16[2,512,1536]{2,1,0:T(8,128)(2,1)} %bitcast.135, bf16[512,1536,1]{1,0,2:T(8,128)(2,1)} %reshape.117), kind=kOutput, calls=%fused_computation.16 | convolution fusion | flops 1610612736 | bytes 6815744 | tf_op jit(solution)/shard_map/dot_general | solution.py:55
  80.4 3.2 %convolution_bitcast_fusion.1 = f32[1,2,512,512]{3,2,1,0:T(8,128)} fusion(bf16[2,512,1536]{2,1,0:T(8,128)(2,1)S(1)} %bitcast.137, bf16[512,1536,1]{1,0,2:T(8,128)(2,1)S(1)} %copy-done.11), kind=kOutput, calls=%fused_computation.15 | convolution fusion | flops 1610612736 | bytes 6815744 | tf_op jit(solution)/shard_map/dot_general | solution.py:55
  83.6 1.6 copy.38
  85.2 1.7 copy.39
  86.9 2.8 %subtract_reduce_fusion = (bf16[512,3,2,128]{3,0,2,1:T(8,128)(2,1)S(1)}, bf16[512,3,2,128]{3,0,2,1:T(8,128)(2,1)S(1)}) fusion(f32[512,3,2,128]{3,0,2,1:T(8,128)} %copy.39, f32[3,3,2,128]{3,2,1,0:T(2,128)S(1)} %copy-done.14, f32[512,3,2,128]{3,0,2,1:T(8,128)S(1)} %copy-done.4, f32[3,3,2,128]{3,2,1,0:T(2,128)S(1)} %get-tuple-element.42), kind=kLoop, calls=%fused_computation.3 | loop fusion | flops 8650752 | bytes 4737024 | tf_op jit(solution)/shard_map/reduce_sum | solution.py:21
  89.9 1.6 copy.40
  92.2 3.9 %convolution_bitcast_fusion = f32[1,2,512,512]{3,2,1,0:T(8,128)S(1)} fusion(bf16[2,512,1536]{2,1,0:T(8,128)(2,1)} %bitcast.136, bf16[512,1536,1]{1,0,2:T(8,128)(2,1)S(1)} %reshape.119), kind=kOutput, calls=%fused_computation.14 | convolution fusion | flops 1610612736 | bytes 6815744 | tf_op jit(solution)/shard_map/dot_general | solution.py:55
  97.4 3.7 %fusion.15 = (f32[3,1,512,512]{3,2,1,0:T(8,128)}, f32[3,512,512]{2,1,0:T(8,128)}) fusion(f32[3,2,512,512]{3,2,1,0:T(8,128)S(1)} %maximum_multiply_fusion), kind=kLoop, calls=%fused_computation.69 | loop fusion | bytes 12582912 | tf_op jit(solution)/shard_map/slice | solution.py:60
  101.9 2.4 copy.43
  104.3 3.5 %copy.47 = f32[3,1,512,512]{2,3,0,1:T(8,128)} copy(f32[3,1,512,512]{3,2,1,0:T(8,128)} %get-tuple-element.16) | data formatting | bytes 6291456
  107.8 5.3 %fusion = (f32[3,1,512,512]{3,2,0,1:T(8,128)S(1)}, f32[3,1,512,512]{3,2,0,1:T(8,128)S(1)}) fusion(f32[3,1,512,512]{2,3,0,1:T(8,128)} %copy.47, f32[3,2,512,512]{3,2,1,0:T(8,128)} %copy-done, f32[3,512,512]{1,2,0:T(8,128)S(1)} %copy.43), kind=kLoop, calls=%fused_computation.11 | loop fusion | flops 1572864 | bytes 18874368 | tf_op jit(solution)/shard_map/stack | solution.py:62
  113.2 3.4 %pad_maximum_fusion = f32[3,2,512,512]{3,2,0,1:T(8,128)} fusion(f32[3,1,512,512]{3,2,0,1:T(8,128)S(1)} %get-tuple-element.15, f32[3,1,512,512]{3,2,0,1:T(8,128)S(1)} %get-tuple-element.14), kind=kLoop, calls=%fused_computation.1 | loop fusion | flops 1572864 | bytes 12582912 | tf_op jit(solution)/shard_map/stack | solution.py:62
  117.3 30.8 %all_gather.7 = bf16[2,512,64]{2,1,0:T(8,128)(2,1)S(1)} all-gather(bf16[2,64,64]{2,1,0:T(8,128)(2,1)S(1)} %copy-done.19), channel_id=1, replica_groups=mesh['grp'=1,'wide'=8,'narrow'=4] {'wide'}, dimensions={1}, use_global_device_ids=true | all-gather | bytes 147456 | tf_op jit(solution)/shard_map/all_gather | solution.py:71
  148.4 79.9 %reduce-scatter.2.cloned.1.call-done = f32[3,2,16,512]{3,2,0,1:T(8,128)} async-done(((f32[3,2,512,512]{3,2,0,1:T(8,128)}), f32[3,2,16,512]{3,2,0,1:T(8,128)}) %reduce-scatter.2.cloned.1.call-update) | async-done | bytes 196624 | tf_op jit(solution)/shard_map/reduce_scatter | solution.py:66
  228.4 8.9 %all_gather.6 = f32[3,2,64,512]{3,2,0,1:T(8,128)S(1)} all-gather(f32[3,2,16,512]{3,2,0,1:T(8,128)} %reduce-scatter.2.cloned.1.call-done), channel_id=1, replica_groups=mesh['grp'=1,'wide'=8,'narrow'=4] {'narrow'}, dimensions={2}, use_global_device_ids=true | all-gather | bytes 983040 | tf_op jit(solution)/shard_map/all_gather | solution.py:67
  (73 shorter events, 18.5 us)
Async XLA Ops:
  7.2 221.2 %reduce-scatter.2.cloned.1.call-start = ((), (), s32[]{:S(2)}) async-start(), calls=%async_computation.1 | async-start | bytes 6488064 | tf_op jit(solution)/shard_map/reduce_scatter | solution.py:66
  12.1 7.7 %copy-start.20 = (s32[3]{0:T(128)S(1)}, s32[3]{0:T(128)}, u32[]{:S(2)}) copy-start(s32[3]{0:T(128)} %param.6) | copy-start | bytes 40
  12.1 11.9 %copy-start.1 = (bf16[512,2,3,2,128]{4,3,2,1,0:T(2,128)(2,1)S(1)}, bf16[512,2,3,2,128]{4,3,2,1,0:T(2,128)(2,1)}, u32[]{:S(2)}) copy-start(bf16[512,2,3,2,128]{4,3,2,1,0:T(2,128)(2,1)} %param.4) | copy-start | bytes 4718596
  12.1 28.5 %collective-permute-start = (bf16[512,2,3,1,128]{0,4,3,2,1:T(8,128)(2,1)}, bf16[512,2,3,1,128]{0,4,3,2,1:T(8,128)(2,1)}, u32[]{:S(2)}, u32[]{:S(2)}) collective-permute-start(bf16[512,2,3,1,128]{0,4,3,2,1:T(8,128)(2,1)} %get-tuple-element.28), channel_id=1, source_target_pairs={{0,28},{4,0},{8,4},{12,8},{16,12},{20,16},{24,20},{28,24},{1,29},{... | collective-permute-start | bytes 2359304 | tf_op jit(solution)/shard_map/ppermute | solution.py:13
  18.2 22.5 %collective-permute-start.1 = (bf16[512,2,3,2,16]{0,4,3,2,1:T(8,128)(2,1)S(1)}, bf16[512,2,3,2,16]{0,4,3,2,1:T(8,128)(2,1)S(1)}, u32[]{:S(2)}, u32[]{:S(2)}) collective-permute-start(bf16[512,2,3,2,16]{0,4,3,2,1:T(8,128)(2,1)S(1)} %slice.148), channel_id=1, source_target_pairs={{0,3},{1,0},{2,1},{3,2},{4,7},{5,4},{6,5},{7,6},{8,11},{9,8},{10,9... | collective-permute-start | bytes 589832 | tf_op jit(solution)/shard_map/ppermute | solution.py:13
  25.2 3.2 %copy-start.13 = (f32[3,2,3,3,2,128]{5,4,3,2,1,0:T(2,128)S(1)}, f32[3,2,3,3,2,128]{5,4,3,2,1,0:T(2,128)}, u32[]{:S(2)}) copy-start(f32[3,2,3,3,2,128]{5,4,3,2,1,0:T(2,128)} %param.5) | copy-start | bytes 165892
  31.9 1.8 copy-start.2
  33.7 2.9 %copy-start.3 = (bf16[512,1536]{1,0:T(8,128)(2,1)S(1)}, bf16[512,1536]{1,0:T(8,128)(2,1)}, u32[]{:S(2)}) copy-start(bf16[512,1536]{1,0:T(8,128)(2,1)} %reshape.106) | copy-start | bytes 4718596
  36.6 3.4 %copy-start.12 = (f32[1,2,3,3,2,128]{5,4,3,2,1,0:T(2,128)S(1)}, f32[1,2,3,3,2,128]{5,4,3,2,1,0:T(2,128)}, u32[]{:S(2)}) copy-start(f32[1,2,3,3,2,128]{5,4,3,2,1,0:T(2,128)} %get-tuple-element.35) | copy-start | bytes 55300
  36.6 4.1 %copy-start.5 = (bf16[512,2,3,2,8,16]{0,5,4,3,2,1:T(8,128)(2,1)S(1)}, bf16[512,2,3,2,8,16]{0,5,4,3,2,1:T(8,128)(2,1)}, u32[]{:S(2)}) copy-start(bf16[512,2,3,2,8,16]{0,5,4,3,2,1:T(8,128)(2,1)} %pad_maximum_fusion.5) | copy-start | bytes 4718596
  36.6 4.1 %copy-start.6 = (bf16[512,2,3,2,112]{0,4,3,2,1:T(8,128)(2,1)S(1)}, bf16[512,2,3,2,112]{0,4,3,2,1:T(8,128)(2,1)}, u32[]{:S(2)}) copy-start(bf16[512,2,3,2,112]{0,4,3,2,1:T(8,128)(2,1)} %slice.147) | copy-start | bytes 4128772
  36.6 4.1 %copy-start.8 = (bf16[512,2,3,1,128]{0,4,3,2,1:T(8,128)(2,1)S(1)}, bf16[512,2,3,1,128]{0,4,3,2,1:T(8,128)(2,1)}, u32[]{:S(2)}) copy-start(bf16[512,2,3,1,128]{0,4,3,2,1:T(8,128)(2,1)} %get-tuple-element.27) | copy-start | bytes 2359300
  46.3 1.9 copy-start.17
  46.3 1.9 copy-start.18
  60.5 3.1 %copy-start.15 = (f32[3,3,2,128]{3,2,1,0:T(2,128)S(1)}, f32[3,3,2,128]{3,2,1,0:T(2,128)}, u32[]{:S(2)}) copy-start(f32[3,3,2,128]{3,2,1,0:T(2,128)} %get-tuple-element.49) | copy-start | bytes 27652
  60.5 3.1 %copy-start.16 = (f32[3,3,2,128]{3,2,1,0:T(2,128)S(1)}, f32[3,3,2,128]{3,2,1,0:T(2,128)}, u32[]{:S(2)}) copy-start(f32[3,3,2,128]{3,2,1,0:T(2,128)} %get-tuple-element.50) | copy-start | bytes 27652
  74.7 5.7 %copy-start.7 = (bf16[1024,1536]{1,0:T(8,128)(2,1)S(1)}, bf16[1024,1536]{1,0:T(8,128)(2,1)}, u32[]{:S(2)}) copy-start(bf16[1024,1536]{1,0:T(8,128)(2,1)} %pad_maximum_fusion.1) | copy-start | bytes 9437188
  74.7 5.7 %copy-start.11 = (bf16[512,1536,1]{1,0,2:T(8,128)(2,1)S(1)}, bf16[512,1536,1]{1,0,2:T(8,128)(2,1)}, u32[]{:S(2)}) copy-start(bf16[512,1536,1]{1,0,2:T(8,128)(2,1)} %reshape.118) | copy-start | bytes 4718596
  85.2 1.7 copy-start.4
  85.2 1.7 copy-start.14
  92.2 3.9 %copy-start.9 = (f32[1,2,512,512]{3,2,1,0:T(8,128)S(1)}, f32[1,2,512,512]{3,2,1,0:T(8,128)}, u32[]{:S(2)}) copy-start(f32[1,2,512,512]{3,2,1,0:T(8,128)} %convolution_bitcast_fusion.2) | copy-start | bytes 6291460
  92.2 3.9 %copy-start.10 = (f32[1,2,512,512]{3,2,1,0:T(8,128)S(1)}, f32[1,2,512,512]{3,2,1,0:T(8,128)}, u32[]{:S(2)}) copy-start(f32[1,2,512,512]{3,2,1,0:T(8,128)} %convolution_bitcast_fusion.1) | copy-start | bytes 6291460
  97.4 4.6 %copy-start = (f32[3,2,512,512]{3,2,1,0:T(8,128)}, f32[3,2,512,512]{3,2,1,0:T(8,128)S(1)}, u32[]{:S(2)}) copy-start(f32[3,2,512,512]{3,2,1,0:T(8,128)S(1)} %maximum_multiply_fusion) | copy-start | bytes 18874372
  116.5 0.8 copy-start.19
Sparse Core Ops, SparseCore 0:
  116.7 111.6 reduce-scatter.1
where the time goes:
time: 247 us; the launch traced here: 246 us
  waiting for transfers between devices  79.9 us (32%)
  local copies, waits for them, and re-layouts  50.1 us (20%)
  blocking collectives  39.7 us (16%)
  other arithmetic  37.9 us (15%)
  between operations  18 us (7%)
  matrix products  13.7 us (6%)
  starting transfers between devices  6.77 us (3%)
    reduce_scatter x1, waiting for transfers between devices, on_device(): lax.psum_scatter(local_terms, ('wide', 'narrow'), scatter_dimension=2, ti...  79.9 us
    all_gather x1, blocking collectives, on_device(): piece = lax.all_gather(peram, 'wide', axis=1, tiled=True)  30.8 us
    mul x8, local copies, waits for them, and re-layouts, covariant_product(): out_real = jnp.sum(link_real * vec_real - link_imag * vec_imag, axis=2)  13.8 us
    dot_general x3, matrix products, on_device(): lax.dot_general(left_block, product, (((1,), (1,)), ((), ())), preferred_...  12.7 us
    unnamed x45, local copies, waits for them, and re-layouts  9.99 us
    all_gather x1, blocking collectives, on_device(): elementals = lax.all_gather(thin_rows, 'narrow', axis=2, tiled=True)  8.85 us
    another operation x2, other arithmetic, on_device(): jnp.stack([real_part - jnp.swapaxes(real_part, 1, 2), imag_part + jnp.swa...  8.68 us
    reduce_sum x3, other arithmetic, covariant_product(): out_real = jnp.sum(link_real * vec_real - link_imag * vec_imag, axis=2)  7.61 us
  transfers between devices with their start and end apart: 3, of which 1 were waited for; matrix products, arithmetic and copies ran while one was open for 7% of the time, Pallas kernels for 0%

commit v1 on v0

v1 whole, which is shorter than its diff:
```python
import functools
import math

import jax
import jax.numpy as jnp
from jax import lax
from jax.experimental import pallas as pl
from jax.experimental.pallas import tpu as pltpu
from jax.sharding import PartitionSpec as P

LZ = 16
ORDER = (2, 1, 0)
CHUNK = 32
MESH = pl.DeviceIdType.MESH
NT = (((1,), (1,)), ((), ()))


def kernel(wides, narrows, norm, vec, links, dirs, peram, elem_out, prod_out,
           pack, halo0, halo1, f_re, f_im, half, part, got_core, got_row, got_wide,
           thin, full, prods, per_all,
           h_send, h_recv, p_send, p_recv, c_send, c_recv, r_send, r_recv,
           w_send, w_recv, g_send, g_recv):
    planes, comps, count, lanes = vec.shape
    groups = lanes // LZ
    per_group = count // groups
    rows = count // wides
    share = 2 * rows // narrows
    across = narrows // 2
    me_w = lax.axis_index("wide")
    me_n = lax.axis_index("narrow")
    core = lax.rem(me_n, 2)
    me_x = me_n // 2

    def at_wide(step):
        return {"wide": lax.rem(me_w + step, wides)}

    def at_narrow(step):
        return {"narrow": lax.rem(me_n + step, narrows)}

    def at_row(step):
        return {"narrow": lax.rem(me_x + step, across) * 2 + core}

    def copy(src, dst, send, recv, where):
        return pltpu.make_async_remote_copy(
            src_ref=src, dst_ref=dst, send_sem=send, recv_sem=recv,
            device_id=where, device_id_type=MESH)

    barrier = pltpu.get_barrier_semaphore()
    for step in range(1, wides):
        pl.semaphore_signal(barrier, inc=1, device_id=at_wide(step), device_id_type=MESH)
    for step in range(1, narrows):
        pl.semaphore_signal(barrier, inc=1, device_id=at_narrow(step), device_id_type=MESH)

    lane = lax.broadcasted_iota(jnp.int32, (CHUNK, lanes), 1)

    def pack_rows(i, carry):
        slab = i // (per_group // CHUNK)
        start = pl.multiple_of(lax.rem(i, per_group // CHUNK) * CHUNK, CHUNK)
        plane = slab // comps
        comp = lax.rem(slab, comps)
        total = jnp.zeros((CHUNK, lanes), jnp.float32)
        for group in range(groups):
            piece = vec[plane, comp, pl.ds(group * per_group + start, CHUNK), :].astype(jnp.float32)
            if group:
                piece = pltpu.roll(piece, group * LZ, 1)
            total = jnp.where(lane // LZ == group, piece, total)
        pack[plane, comp, pl.ds(start, CHUNK), :] = total.astype(jnp.bfloat16)
        return carry

    lax.fori_loop(0, planes * comps * (per_group // CHUNK), pack_rows, 0)

    pl.semaphore_wait(barrier, wides + narrows - 2)
    first_copy = copy(vec.at[0], halo0, h_send.at[0], h_recv.at[0], at_wide(wides - 1))
    second_copy = copy(pack, halo1, h_send.at[1], h_recv.at[1], at_narrow(narrows - 1))
    second_copy.start()
    first_copy.start()
    per_copies = [
        copy(peram, per_all.at[me_w], p_send.at[step - 1], p_recv.at[step - 1], at_wide(step))
        for step in range(1, wides)
    ]
    for one in per_copies:
        one.start()
    per_all[me_w] = peram[...]

    def shifted(direction, plane, comp, start):
        here = pl.ds(start, CHUNK)
        if direction == 0:
            if plane + 1 < planes:
                return vec[plane + 1, comp, here, :].astype(jnp.float32)
            return halo0[comp, here, :].astype(jnp.float32)
        own = vec[plane, comp, here, :].astype(jnp.float32)
        if direction == 1:
            group = start // per_group
            inside = pl.multiple_of(lax.rem(start, per_group), CHUNK)
            ahead = halo1[plane, comp, pl.ds(inside, CHUNK), :].astype(jnp.float32)
            ahead = pltpu.roll(ahead, lanes - LZ - LZ * group, 1)
            return jnp.where(lane < lanes - LZ, pltpu.roll(own, lanes - LZ, 1), ahead)
        return jnp.where(
            lax.rem(lane, LZ) < LZ - 1, pltpu.roll(own, lanes - 1, 1), pltpu.roll(own, LZ - 1, 1))

    def forward(direction):
        for plane in range(planes):
            def chunk(i, carry):
                start = pl.multiple_of(i * CHUNK, CHUNK)
                values = [shifted(direction, plane, comp, start) for comp in range(comps)]
                for a in range(3):
                    real = imag = None
                    for b in range(3):
                        link_r = links[direction, 0, a, b, plane:plane + 1, :]
                        link_i = links[direction, 1, a, b, plane:plane + 1, :]
                        term_r = link_r * values[b] - link_i * values[3 + b]
                        term_i = link_r * values[3 + b] + link_i * values[b]
                        real = term_r if real is None else real + term_r
                        imag = term_i if imag is None else imag + term_i
                    real = real.astype(jnp.bfloat16)
                    imag = imag.astype(jnp.bfloat16)
                    low = (plane * comps + a) * lanes
                    high = low + 3 * lanes
                    f_re[pl.ds(start, CHUNK), low:low + lanes] = real
                    f_re[pl.ds(start, CHUNK), high:high + lanes] = imag
                    f_im[pl.ds(start, CHUNK), low:low + lanes] = imag
                    f_im[pl.ds(start, CHUNK), high:high + lanes] = -real
                return carry

            lax.fori_loop(0, count // CHUNK, chunk, 0)

    def compute(direction):
        forward(direction)
        left = jnp.concatenate(
            [vec[plane, comp] for plane in range(planes) for comp in range(comps)], 1)
        half[0] = lax.dot_general(left, f_re[...], NT, preferred_element_type=jnp.float32)
        half[1] = lax.dot_general(left, f_im[...], NT, preferred_element_type=jnp.float32)
        block = lanes
        for c in range(2):
            for top in range(0, count, block):
                turned = half[c, :, top:top + block].T
                own = half[c, top:top + block, :]
                terms = ((own - turned) if c == 0 else (own + turned)) * norm
                for low in range(0, block, share):
                    row = top + low
                    owner = c * across + (row % rows) // share
                    part[direction, owner % 2, owner // 2, row // rows] = (
                        terms[low:low + share].astype(jnp.bfloat16))

    def core_copy(d):
        return copy(part.at[d, 1 - core], got_core.at[d], c_send.at[d], c_recv.at[d],
                    {"narrow": me_x * 2 + 1 - core})

    def row_copy(d, step):
        return copy(part.at[d, core, lax.rem(me_x + step, across)], got_row.at[d, step - 1],
                    r_send.at[d, step - 1], r_recv.at[d, step - 1], at_row(step))

    def wide_copy(d, step):
        return copy(part.at[d, core, me_x, lax.rem(me_w + step, wides)],
                    got_wide.at[d, step - 1],
                    w_send.at[d, step - 1], w_recv.at[d, step - 1], at_wide(step))

    def full_copy(d, step):
        return copy(thin.at[d], full.at[d, me_n], g_send.at[d, step - 1], g_recv.at[d, step - 1],
                    at_narrow(step))

    def core_done(d):
        core_copy(d).wait()
        for x in range(across):
            def add(w, carry):
                part[d, core, x, w] = (
                    part[d, core, x, w].astype(jnp.float32)
                    + got_core[d, x, w].astype(jnp.float32)).astype(jnp.bfloat16)
                return carry
            lax.fori_loop(0, wides, add, 0)
        for step in range(1, across):
            row_copy(d, step).start()

    def row_done(d):
        for step in range(1, across):
            row_copy(d, step).wait()

        def add(w, carry):
            total = part[d, core, me_x, w].astype(jnp.float32)
            for step in range(1, across):
                total = total + got_row[d, step - 1, w].astype(jnp.float32)
            part[d, core, me_x, w] = total.astype(jnp.bfloat16)
            return carry

        lax.fori_loop(0, wides, add, 0)
        for step in range(1, wides):
            wide_copy(d, step).start()

    def wide_done(d):
        for step in range(1, wides):
            wide_copy(d, step).wait()
        total = part[d, core, me_x, me_w].astype(jnp.float32)
        for step in range(1, wides):
            total = total + got_wide[d, step - 1].astype(jnp.float32)
        total = total.astype(jnp.bfloat16)
        thin[d] = total
        full[d, me_n] = total
        for step in range(1, narrows):
            full_copy(d, step).start()

    def finish(d):
        for step in range(1, narrows):
            full_copy(d, step).wait()
        real = full[d, 0:across].astype(jnp.float32).reshape(rows, count).astype(jnp.bfloat16)
        imag = full[d, across:narrows].astype(jnp.float32).reshape(rows, count).astype(jnp.bfloat16)
        per_r = per_all[:, 0].reshape(count, per_all.shape[3])
        per_i = per_all[:, 1].reshape(count, per_all.shape[3])

        def times(x, y):
            return jnp.dot(x, y, preferred_element_type=jnp.float32)

        prods[d, 0] = times(real, per_r) - times(imag, per_i)
        prods[d, 1] = times(real, per_i) + times(imag, per_r)

    compute(2)
    core_copy(2).start()
    second_copy.wait()
    compute(1)
    core_copy(1).start()
    core_done(2)
    first_copy.wait()
    compute(0)
    core_copy(0).start()
    row_done(2)
    core_done(1)
    core_done(0)
    row_done(1)
    wide_done(2)
    row_done(0)
    for one in per_copies:
        one.wait()
    wide_done(1)
    finish(2)
    wide_done(0)
    finish(1)
    finish(0)
    for slot in range(3):
        d = dirs[slot]
        elem_out[slot] = full[d].astype(jnp.float32).reshape(2, rows, count)
        prod_out[slot] = prods[d]


def on_device(vectors, links, directions, peram):
    count, _, _, planes, lanes = vectors.shape
    wides = lax.axis_size("wide")
    narrows = lax.axis_size("narrow")
    slots = directions.shape[0]
    cols = peram.shape[2]
    rows = count // wides
    share = 2 * rows // narrows
    across = narrows // 2
    norm = 1.0 / math.sqrt(12.0 * planes * wides * lanes * narrows)
    turned = vectors.transpose(3, 1, 2, 0, 4).reshape(planes, 6, count, lanes)
    vmem = pl.BlockSpec(memory_space=pltpu.VMEM)
    low = jnp.bfloat16
    dma = pltpu.SemaphoreType.DMA
    return pl.pallas_call(
        functools.partial(kernel, wides, narrows, norm),
        out_shape=(
            jax.ShapeDtypeStruct((slots, 2, rows, count), jnp.float32),
            jax.ShapeDtypeStruct((slots, 2, rows, cols), jnp.float32),
        ),
        in_specs=[vmem, vmem, pl.BlockSpec(memory_space=pltpu.SMEM), vmem],
        out_specs=(vmem, vmem),
        scratch_shapes=[
            pltpu.VMEM((planes, 6, count * LZ // lanes, lanes), low),
            pltpu.VMEM((6, count, lanes), low),
            pltpu.VMEM((planes, 6, count * LZ // lanes, lanes), low),
            pltpu.VMEM((count, planes * 6 * lanes), low),
            pltpu.VMEM((count, planes * 6 * lanes), low),
            pltpu.VMEM((2, count, count), jnp.float32),
            pltpu.VMEM((3, 2, across, wides, share, count), low),
            pltpu.VMEM((3, across, wides, share, count), low),
            pltpu.VMEM((3, across - 1, wides, share, count), low),
            pltpu.VMEM((3, wides - 1, share, count), low),
            pltpu.VMEM((3, share, count), low),
            pltpu.VMEM((3, narrows, share, count), low),
            pltpu.VMEM((3, 2, rows, cols), jnp.float32),
            pltpu.VMEM((wides, 2, rows, cols), low),
            dma((2,)), dma((2,)),
            dma((wides - 1,)), dma((wides - 1,)),
            dma((3,)), dma((3,)),
            dma((3, across - 1)), dma((3, across - 1)),
            dma((3, wides - 1)), dma((3, wides - 1)),
            dma((3, narrows - 1)), dma((3, narrows - 1)),
        ],
        compiler_params=pltpu.CompilerParams(
            collective_id=0, has_side_effects=True, vmem_limit_bytes=50 * 2**20),
    )(turned, links, directions, peram)


def solution(mesh):
    placed = (
        P("grp", None, None, "wide", "narrow"),
        P("grp", None, None, None, "wide", "narrow"),
        P(),
        P("grp", "wide", "narrow"),
    )
    return jax.shard_map(
        on_device,
        mesh=mesh,
        in_specs=placed,
        out_specs=(P("grp", None, "wide", None), P("grp", None, "wide", "narrow")),
        check_vma=False,
    )
```

time: 247 us -> 57.5 us (0.23)
  waiting for transfers between devices: 79.9 us -> 0 us
  Pallas kernels: 0 us -> 53.3 us
  local copies, waits for them, and re-layouts: 50.1 us -> 3.29 us
  blocking collectives: 39.7 us -> 0 us
  other arithmetic: 37.9 us -> 0 us
  between operations: 18 us -> 0.69 us
  matrix products: 13.7 us -> 0 us
  starting transfers between devices: 6.77 us -> 0 us
    reduce_scatter x1 -> x0, waiting for transfers between devices: 79.9 us -> none  [on_device(): lax.psum_scatter(local_terms, ('wide', 'narrow'), scatter_dimension=2, ti...]
    pallas_call x0 -> x1, Pallas kernels: none -> 53.3 us  [on_device(): pl.pallas_call(functools.partial(kernel, wides, narrows, norm), out_shape...]
    all_gather x2 -> x0, blocking collectives: 39.7 us -> none  [the longest x1 30.8 us: on_device(): piece = lax.all_gather(peram, 'wide', axis=1, tiled=True)]
    mul x8 -> x0, local copies, waits for them, and re-layouts: 13.8 us -> none  [covariant_product(): out_real = jnp.sum(link_real * vec_real - link_imag * vec_imag, axis=2)]
    dot_general x4 -> x0, matrix products: 13.7 us -> none  [the longest x3 12.7 us: on_device(): lax.dot_general(left_block, product, (((1,), (1,)), ((), ())), preferred_...]
    another operation x5 -> x0, other arithmetic: 9.12 us -> none  [the longest x2 8.68 us: on_device(): jnp.stack([real_part - jnp.swapaxes(real_part, 1, 2), imag_part + jnp.swa...]
    unnamed x45 -> x8, local copies, waits for them, and re-layouts: 9.99 us -> 1.57 us
    concatenate x3 -> x0, other arithmetic: 8.31 us -> none  [the longest x1 3.41 us: on_device(): jnp.concatenate([vectors.reshape(vec_count, -1), rotated.reshape(vec_coun...]
  transfers between devices with their start and end apart: 3 -> 0, of which waited for: 1 -> 0; matrix products, arithmetic and copies ran while one was open for 7% -> 0% of each run, Pallas kernels for 0% -> 0%
where the time goes in v1:
time: 57.5 us; the launch traced here: 57.3 us
  Pallas kernels  53.3 us (93%)
  local copies, waits for them, and re-layouts  3.29 us (6%)
  between operations  0.69 us (1%)
    pallas_call x1, Pallas kernels, on_device(): pl.pallas_call(functools.partial(kernel, wides, narrows, norm), out_shape...  53.3 us
    transpose x1, local copies, waits for them, and re-layouts, on_device(): turned = vectors.transpose(3, 1, 2, 0, 4).reshape(planes, 6, count, lanes)  1.72 us
    unnamed x8, local copies, waits for them, and re-layouts  1.57 us

profile of v1, /device:TPU:0, one launch (start us, length us, event | category | flops | bytes accessed | tf_op | source)
XLA Modules:
  0.0 57.3 jit_solution(9204154749802221226)
XLA Ops:
  0.6 0.0 copy-start
  0.6 0.0 copy-start.1
  0.7 0.0 copy-start.2
  0.7 1.7 %copy.6 = bf16[2,2,3,512,128]{4,3,2,1,0:T(8,128)(2,1)S(1)} copy(bf16[2,2,3,512,128]{4,0,2,1,3:T(2,128)(2,1)} %bitcast.3) | data formatting | bytes 3145728 | tf_op jit(solution)/shard_map/transpose | solution.py:253
  2.4 0.0 copy-done
  2.4 0.0 copy-done.1
  2.4 0.0 copy-done.2
  2.4 53.3 %shard_map.59 = (f32[3,2,64,512]{3,2,1,0:T(8,128)S(1)}, f32[3,2,64,64]{3,2,1,0:T(8,128)S(1)}) custom-call(bf16[2,6,512,128]{3,2,1,0:T(8,128)(2,1)S(1)} %bitcast.2, f32[3,2,3,3,2,128]{5,4,3,2,1,0:T(2,128)S(1)} %copy-done, s32[3]{0:T(128)S(1)} %copy-done.2, bf16[2,64,64]{2,1,0:T(8,128)(2,1)S(1)} %copy-done.1), custom_call_target="tpu_custom_call" | custom-call | tf_op jit(solution)/shard_map/pallas_call | solution.py:257
  55.8 0.9 %copy.9 = f32[3,2,64,512]{3,2,1,0:T(8,128)} copy(f32[3,2,64,512]{3,2,1,0:T(8,128)S(1)} %get-tuple-element.4) | data formatting | bytes 1572864
  56.7 0.7 %copy.10 = f32[3,2,64,64]{3,2,1,0:T(8,128)} copy(f32[3,2,64,64]{3,2,1,0:T(8,128)S(1)} %get-tuple-element.5) | data formatting | bytes 196608
Async XLA Ops:
  0.6 1.8 %copy-start = (f32[3,2,3,3,2,128]{5,4,3,2,1,0:T(2,128)S(1)}, f32[3,2,3,3,2,128]{5,4,3,2,1,0:T(2,128)}, u32[]{:S(2)}) copy-start(f32[3,2,3,3,2,128]{5,4,3,2,1,0:T(2,128)} %links.1) | copy-start | bytes 165892
  0.6 1.8 %copy-start.1 = (bf16[2,64,64]{2,1,0:T(8,128)(2,1)S(1)}, bf16[2,64,64]{2,1,0:T(8,128)(2,1)}, u32[]{:S(2)}) copy-start(bf16[2,64,64]{2,1,0:T(8,128)(2,1)} %peram.1) | copy-start | bytes 49156
  0.7 1.8 %copy-start.2 = (s32[3]{0:T(128)S(1)}, s32[3]{0:T(128)}, u32[]{:S(2)}) copy-start(s32[3]{0:T(128)} %dirs.1) | copy-start | bytes 40

commit v2 on v1

--- a/solution.py
+++ b/solution.py
@@ -9,17 +9,17 @@
 from jax.sharding import PartitionSpec as P
 
 LZ = 16
-ORDER = (2, 1, 0)
+PIECES = 4
 CHUNK = 32
 MESH = pl.DeviceIdType.MESH
 NT = (((1,), (1,)), ((), ()))
 
 
 def kernel(wides, narrows, norm, vec, links, dirs, peram, elem_out, prod_out,
-           pack, halo0, halo1, f_re, f_im, half, part, got_core, got_row, got_wide,
-           thin, full, prods, per_all,
-           h_send, h_recv, p_send, p_recv, c_send, c_recv, r_send, r_recv,
-           w_send, w_recv, g_send, g_recv):
+           pack, halo0, halo1, f_re, f_im, half, keep, part, got_core, got_row, got_wide,
+           got_all, thin, full, prods, per_all,
+           h_send, h_recv, s_send, s_recv, p_send, p_recv, c_send, c_recv, r_send, r_recv,
+           w_send, w_recv, a_send, a_recv, g_send, g_recv):
     planes, comps, count, lanes = vec.shape
     groups = lanes // LZ
     per_group = count // groups
@@ -37,8 +37,8 @@
     def at_narrow(step):
         return {"narrow": lax.rem(me_n + step, narrows)}
 
-    def at_row(step):
-        return {"narrow": lax.rem(me_x + step, across) * 2 + core}
+    def at_chip(x, step):
+        return {"wide": lax.rem(me_w + step, wides), "narrow": x * 2 + core}
 
     def copy(src, dst, send, recv, where):
         return pltpu.make_async_remote_copy(
@@ -46,12 +46,28 @@
             device_id=where, device_id_type=MESH)
 
     barrier = pltpu.get_barrier_semaphore()
-    for step in range(1, wides):
-        pl.semaphore_signal(barrier, inc=1, device_id=at_wide(step), device_id_type=MESH)
-    for step in range(1, narrows):
-        pl.semaphore_signal(barrier, inc=1, device_id=at_narrow(step), device_id_type=MESH)
+
+    def greet(where):
+        pl.semaphore_signal(barrier, inc=1, device_id=where, device_id_type=MESH)
+
+    for x_step in range(across):
+        for w_step in range(wides):
+            if x_step or w_step:
+                greet(at_chip(lax.rem(me_x + x_step, across), w_step))
+        greet({"narrow": lax.rem(me_x + x_step, across) * 2 + 1 - core})
 
     lane = lax.broadcasted_iota(jnp.int32, (CHUNK, lanes), 1)
+
+    pl.semaphore_wait(barrier, across * wides - 1 + across)
+    pieces = h_send.shape[0]
+    depth = count // pieces
+    halo_copies = [
+        copy(vec.at[0, :, pl.ds(piece * depth, depth)], halo0.at[:, pl.ds(piece * depth, depth)],
+             h_send.at[piece], h_recv.at[piece], at_wide(wides - 1))
+        for piece in range(pieces)
+    ]
+    for one in halo_copies:
+        one.start()
 
     def pack_rows(i, carry):
         slab = i // (per_group // CHUNK)
@@ -68,12 +84,8 @@
         return carry
 
     lax.fori_loop(0, planes * comps * (per_group // CHUNK), pack_rows, 0)
-
-    pl.semaphore_wait(barrier, wides + narrows - 2)
-    first_copy = copy(vec.at[0], halo0, h_send.at[0], h_recv.at[0], at_wide(wides - 1))
-    second_copy = copy(pack, halo1, h_send.at[1], h_recv.at[1], at_narrow(narrows - 1))
+    second_copy = copy(pack, halo1, s_send.at[0], s_recv.at[0], at_narrow(narrows - 1))
     second_copy.start()
-    first_copy.start()
     per_copies = [
         copy(peram, per_all.at[me_w], p_send.at[step - 1], p_recv.at[step - 1], at_wide(step))
         for step in range(1, wides)
@@ -98,8 +110,8 @@
         return jnp.where(
             lax.rem(lane, LZ) < LZ - 1, pltpu.roll(own, lanes - 1, 1), pltpu.roll(own, LZ - 1, 1))
 
-    def forward(direction):
-        for plane in range(planes):
+    def forward(direction, planes_here, first=0, last=count):
+        for plane in planes_here:
             def chunk(i, carry):
                 start = pl.multiple_of(i * CHUNK, CHUNK)
                 values = [shifted(direction, plane, comp, start) for comp in range(comps)]
@@ -122,76 +134,104 @@
                     f_im[pl.ds(start, CHUNK), high:high + lanes] = -real
                 return carry
 
-            lax.fori_loop(0, count // CHUNK, chunk, 0)
-
-    def compute(direction):
-        forward(direction)
+            lax.fori_loop(first // CHUNK, last // CHUNK, chunk, 0)
+
+    mid = count // 2
+    xs_of = (range(0, across // 2), range(across // 2, across))
+
+    def multiply(c, low, high):
         left = jnp.concatenate(
             [vec[plane, comp] for plane in range(planes) for comp in range(comps)], 1)
-        half[0] = lax.dot_general(left, f_re[...], NT, preferred_element_type=jnp.float32)
-        half[1] = lax.dot_general(left, f_im[...], NT, preferred_element_type=jnp.float32)
+        right = f_re if c == 0 else f_im
+        half[c, :, low:high] = lax.dot_general(
+            left, right[low:high, :], NT, preferred_element_type=jnp.float32)
+
+    def core_copy(d, c):
+        xs = pl.ds(xs_of[c][0], len(xs_of[c]))
+        return copy(keep.at[d, 1 - core, xs], got_core.at[d, xs], c_send.at[d, c],
+                    c_recv.at[d, c], {"narrow": me_x * 2 + 1 - core})
+
+    def balance(d, c):
         block = lanes
-        for c in range(2):
-            for top in range(0, count, block):
-                turned = half[c, :, top:top + block].T
-                own = half[c, top:top + block, :]
-                terms = ((own - turned) if c == 0 else (own + turned)) * norm
-                for low in range(0, block, share):
-                    row = top + low
-                    owner = c * across + (row % rows) // share
-                    part[direction, owner % 2, owner // 2, row // rows] = (
-                        terms[low:low + share].astype(jnp.bfloat16))
-
-    def core_copy(d):
-        return copy(part.at[d, 1 - core], got_core.at[d], c_send.at[d], c_recv.at[d],
-                    {"narrow": me_x * 2 + 1 - core})
-
-    def row_copy(d, step):
-        return copy(part.at[d, core, lax.rem(me_x + step, across)], got_row.at[d, step - 1],
-                    r_send.at[d, step - 1], r_recv.at[d, step - 1], at_row(step))
+        for top in range(0, count, block):
+            turned = half[c, :, top:top + block].T
+            own = half[c, top:top + block, :]
+            terms = ((own - turned) if c == 0 else (own + turned)) * norm
+            for low in range(0, block, share):
+                row = top + low
+                owner = c * across + (row % rows) // share
+                keep[d, owner % 2, owner // 2, row // rows] = terms[low:low + share]
+        core_copy(d, c).start()
+
+    def row_copy(d, x, step):
+        return copy(part.at[d, x], got_row.at[d - 1, step - 1],
+                    r_send.at[d - 1, step - 1], r_recv.at[d - 1, step - 1], at_chip(x, 0))
 
     def wide_copy(d, step):
-        return copy(part.at[d, core, me_x, lax.rem(me_w + step, wides)],
-                    got_wide.at[d, step - 1],
-                    w_send.at[d, step - 1], w_recv.at[d, step - 1], at_wide(step))
+        return copy(part.at[d, me_x, lax.rem(me_w + step, wides)],
+                    got_wide.at[d - 1, step - 1],
+                    w_send.at[d - 1, step - 1], w_recv.at[d - 1, step - 1], at_wide(step))
+
+    def chip_copy(x, x_step, w_step):
+        return copy(part.at[0, x, lax.rem(me_w + w_step, wides)], got_all.at[x_step, w_step],
+                    a_send.at[x_step, w_step], a_recv.at[x_step, w_step], at_chip(x, w_step))
 
     def full_copy(d, step):
         return copy(thin.at[d], full.at[d, me_n], g_send.at[d, step - 1], g_recv.at[d, step - 1],
                     at_narrow(step))
 
-    def core_done(d):
-        core_copy(d).wait()
-        for x in range(across):
+    def push(d, c):
+        core_copy(d, c).wait()
+        for x in xs_of[c]:
             def add(w, carry):
-                part[d, core, x, w] = (
-                    part[d, core, x, w].astype(jnp.float32)
-                    + got_core[d, x, w].astype(jnp.float32)).astype(jnp.bfloat16)
+                total = keep[d, core, x, w] + got_core[d, x, w]
+                keep[d, core, x, w] = total
+                part[d, x, w] = total.astype(jnp.bfloat16)
                 return carry
+
             lax.fori_loop(0, wides, add, 0)
-        for step in range(1, across):
-            row_copy(d, step).start()
+            x_step = lax.rem(x - me_x + across, across)
+            if d:
+                @pl.when(x_step > 0)
+                def _():
+                    row_copy(d, x, x_step).start()
+            else:
+                for w_step in range(1, wides):
+                    chip_copy(x, x_step, w_step).start()
+
+                @pl.when(x_step > 0)
+                def _():
+                    chip_copy(x, x_step, 0).start()
 
     def row_done(d):
         for step in range(1, across):
-            row_copy(d, step).wait()
+            row_copy(d, lax.rem(me_x + step, across), step).wait()
 
         def add(w, carry):
-            total = part[d, core, me_x, w].astype(jnp.float32)
+            total = keep[d, core, me_x, w]
             for step in range(1, across):
-                total = total + got_row[d, step - 1, w].astype(jnp.float32)
-            part[d, core, me_x, w] = total.astype(jnp.bfloat16)
+                total = total + got_row[d - 1, step - 1, w].astype(jnp.float32)
+            keep[d, core, me_x, w] = total
+            part[d, me_x, w] = total.astype(jnp.bfloat16)
             return carry
 
         lax.fori_loop(0, wides, add, 0)
         for step in range(1, wides):
             wide_copy(d, step).start()
 
-    def wide_done(d):
-        for step in range(1, wides):
-            wide_copy(d, step).wait()
-        total = part[d, core, me_x, me_w].astype(jnp.float32)
-        for step in range(1, wides):
-            total = total + got_wide[d, step - 1].astype(jnp.float32)
+    def total_done(d):
+        total = keep[d, core, me_x, me_w]
+        if d:
+            for step in range(1, wides):
+                wide_copy(d, step).wait()
+            for step in range(1, wides):
+                total = total + got_wide[d - 1, step - 1].astype(jnp.float32)
+        else:
+            steps = [(x, w) for x in range(across) for w in range(wides) if x or w]
+            for x_step, w_step in steps:
+                chip_copy(lax.rem(me_x + x_step, across), x_step, w_step).wait()
+            for x_step, w_step in steps:
+                total = total + got_all[x_step, w_step].astype(jnp.float32)
         total = total.astype(jnp.bfloat16)
         thin[d] = total
         full[d, me_n] = total
@@ -212,27 +252,42 @@
         prods[d, 0] = times(real, per_r) - times(imag, per_i)
         prods[d, 1] = times(real, per_i) + times(imag, per_r)
 
-    compute(2)
-    core_copy(2).start()
+    every = range(planes)
+    forward(2, every)
+    for c in range(2):
+        multiply(c, 0, count)
+        balance(2, c)
     second_copy.wait()
-    compute(1)
-    core_copy(1).start()
-    core_done(2)
-    first_copy.wait()
-    compute(0)
-    core_copy(0).start()
-    row_done(2)
-    core_done(1)
-    core_done(0)
+    forward(1, every[:1])
+    push(2, 0)
+    push(2, 1)
+    forward(1, every[1:])
+    for c in range(2):
+        multiply(c, 0, count)
+        balance(1, c)
+    forward(0, every[:-1])
+    push(1, 0)
+    push(1, 1)
+    for piece in range(pieces):
+        halo_copies[piece].wait()
+        forward(0, every[-1:], piece * depth, (piece + 1) * depth)
+        if piece == pieces // 2 - 1:
+            row_done(2)
+            multiply(0, 0, mid)
+            multiply(1, 0, mid)
+    for c in range(2):
+        multiply(c, mid, count)
+        balance(0, c)
     row_done(1)
-    wide_done(2)
-    row_done(0)
+    push(0, 0)
+    push(0, 1)
+    total_done(2)
     for one in per_copies:
         one.wait()
-    wide_done(1)
+    total_done(1)
     finish(2)
-    wide_done(0)
     finish(1)
+    total_done(0)
     finish(0)
     for slot in range(3):
         d = dirs[slot]
@@ -269,19 +324,23 @@
             pltpu.VMEM((count, planes * 6 * lanes), low),
             pltpu.VMEM((count, planes * 6 * lanes), low),
             pltpu.VMEM((2, count, count), jnp.float32),
-            pltpu.VMEM((3, 2, across, wides, share, count), low),
+            pltpu.VMEM((3, 2, across, wides, share, count), jnp.float32),
             pltpu.VMEM((3, across, wides, share, count), low),
-            pltpu.VMEM((3, across - 1, wides, share, count), low),
-            pltpu.VMEM((3, wides - 1, share, count), low),
+            pltpu.VMEM((3, across, wides, share, count), jnp.float32),
+            pltpu.VMEM((2, across - 1, wides, share, count), low),
+            pltpu.VMEM((2, wides - 1, share, count), low),
+            pltpu.VMEM((across, wides, share, count), low),
             pltpu.VMEM((3, share, count), low),
             pltpu.VMEM((3, narrows, share, count), low),
             pltpu.VMEM((3, 2, rows, cols), jnp.float32),
             pltpu.VMEM((wides, 2, rows, cols), low),
-            dma((2,)), dma((2,)),
+            dma((PIECES,)), dma((PIECES,)),
+            dma((1,)), dma((1,)),
             dma((wides - 1,)), dma((wides - 1,)),
-            dma((3,)), dma((3,)),
-            dma((3, across - 1)), dma((3, across - 1)),
-            dma((3, wides - 1)), dma((3, wides - 1)),
+            dma((3, 2)), dma((3, 2)),
+            dma((2, across - 1)), dma((2, across - 1)),
+            dma((2, wides - 1)), dma((2, wides - 1)),
+            dma((across, wides)), dma((across, wides)),
             dma((3, narrows - 1)), dma((3, narrows - 1)),
         ],
         compiler_params=pltpu.CompilerParams(

time: 57.5 us -> 61.5 us (1.070)
  Pallas kernels: 53.3 us -> 57.3 us
    pallas_call x1, Pallas kernels: 53.3 us -> 57.3 us  [on_device(): pl.pallas_call(functools.partial(kernel, wides, narrows, norm), out_shape...]
where the time goes in v2:
time: 61.5 us; the launch traced here: 61.3 us
  Pallas kernels  57.3 us (93%)
  local copies, waits for them, and re-layouts  3.29 us (5%)
  between operations  0.69 us (1%)
    pallas_call x1, Pallas kernels, on_device(): pl.pallas_call(functools.partial(kernel, wides, narrows, norm), out_shape...  57.3 us
    transpose x1, local copies, waits for them, and re-layouts, on_device(): turned = vectors.transpose(3, 1, 2, 0, 4).reshape(planes, 6, count, lanes)  1.72 us
    unnamed x8, local copies, waits for them, and re-layouts  1.57 us

profile of v2, /device:TPU:0, one launch (start us, length us, event | category | flops | bytes accessed | tf_op | source)
XLA Modules:
  0.0 61.3 jit_solution(10475607727627747765)
XLA Ops:
  0.6 0.0 copy-start
  0.6 0.0 copy-start.1
  0.7 0.0 copy-start.2
  0.7 1.7 %copy.6 = bf16[2,2,3,512,128]{4,3,2,1,0:T(8,128)(2,1)S(1)} copy(bf16[2,2,3,512,128]{4,0,2,1,3:T(2,128)(2,1)} %bitcast.3) | data formatting | bytes 3145728 | tf_op jit(solution)/shard_map/transpose | solution.py:308
  2.4 0.0 copy-done
  2.4 0.0 copy-done.1
  2.4 0.0 copy-done.2
  2.4 57.3 %shard_map.59 = (f32[3,2,64,512]{3,2,1,0:T(8,128)S(1)}, f32[3,2,64,64]{3,2,1,0:T(8,128)S(1)}) custom-call(bf16[2,6,512,128]{3,2,1,0:T(8,128)(2,1)S(1)} %bitcast.2, f32[3,2,3,3,2,128]{5,4,3,2,1,0:T(2,128)S(1)} %copy-done, s32[3]{0:T(128)S(1)} %copy-done.2, bf16[2,64,64]{2,1,0:T(8,128)(2,1)S(1)} %copy-done.1), custom_call_target="tpu_custom_call" | custom-call | tf_op jit(solution)/shard_map/pallas_call | solution.py:312
  59.7 0.9 %copy.9 = f32[3,2,64,512]{3,2,1,0:T(8,128)} copy(f32[3,2,64,512]{3,2,1,0:T(8,128)S(1)} %get-tuple-element.4) | data formatting | bytes 1572864
  60.6 0.7 %copy.10 = f32[3,2,64,64]{3,2,1,0:T(8,128)} copy(f32[3,2,64,64]{3,2,1,0:T(8,128)S(1)} %get-tuple-element.5) | data formatting | bytes 196608
Async XLA Ops:
  0.6 1.8 %copy-start = (f32[3,2,3,3,2,128]{5,4,3,2,1,0:T(2,128)S(1)}, f32[3,2,3,3,2,128]{5,4,3,2,1,0:T(2,128)}, u32[]{:S(2)}) copy-start(f32[3,2,3,3,2,128]{5,4,3,2,1,0:T(2,128)} %links.1) | copy-start | bytes 165892
  0.6 1.8 %copy-start.1 = (bf16[2,64,64]{2,1,0:T(8,128)(2,1)S(1)}, bf16[2,64,64]{2,1,0:T(8,128)(2,1)}, u32[]{:S(2)}) copy-start(bf16[2,64,64]{2,1,0:T(8,128)(2,1)} %peram.1) | copy-start | bytes 49156
  0.7 1.8 %copy-start.2 = (s32[3]{0:T(128)S(1)}, s32[3]{0:T(128)}, u32[]{:S(2)}) copy-start(s32[3]{0:T(128)} %dirs.1) | copy-start | bytes 40

commit v3 on v1

--- a/solution.py
+++ b/solution.py
@@ -16,7 +16,7 @@
 
 
 def kernel(wides, narrows, norm, vec, links, dirs, peram, elem_out, prod_out,
-           pack, halo0, halo1, f_re, f_im, half, part, got_core, got_row, got_wide,
+           pack, halo0, halo1, f_re, f_im, half, keep, part, got_core, got_row, got_wide,
            thin, full, prods, per_all,
            h_send, h_recv, p_send, p_recv, c_send, c_recv, r_send, r_recv,
            w_send, w_recv, g_send, g_recv):
@@ -139,8 +139,9 @@
                 for low in range(0, block, share):
                     row = top + low
                     owner = c * across + (row % rows) // share
-                    part[direction, owner % 2, owner // 2, row // rows] = (
-                        terms[low:low + share].astype(jnp.bfloat16))
+                    piece = terms[low:low + share]
+                    keep[direction, owner % 2, owner // 2, row // rows] = piece
+                    part[direction, owner % 2, owner // 2, row // rows] = piece.astype(jnp.bfloat16)
 
     def core_copy(d):
         return copy(part.at[d, 1 - core], got_core.at[d], c_send.at[d], c_recv.at[d],
@@ -163,9 +164,9 @@
         core_copy(d).wait()
         for x in range(across):
             def add(w, carry):
-                part[d, core, x, w] = (
-                    part[d, core, x, w].astype(jnp.float32)
-                    + got_core[d, x, w].astype(jnp.float32)).astype(jnp.bfloat16)
+                total = keep[d, core, x, w] + got_core[d, x, w].astype(jnp.float32)
+                keep[d, core, x, w] = total
+                part[d, core, x, w] = total.astype(jnp.bfloat16)
                 return carry
             lax.fori_loop(0, wides, add, 0)
         for step in range(1, across):
@@ -176,9 +177,10 @@
             row_copy(d, step).wait()
 
         def add(w, carry):
-            total = part[d, core, me_x, w].astype(jnp.float32)
+            total = keep[d, core, me_x, w]
             for step in range(1, across):
                 total = total + got_row[d, step - 1, w].astype(jnp.float32)
+            keep[d, core, me_x, w] = total
             part[d, core, me_x, w] = total.astype(jnp.bfloat16)
             return carry
 
@@ -189,7 +191,7 @@
     def wide_done(d):
         for step in range(1, wides):
             wide_copy(d, step).wait()
-        total = part[d, core, me_x, me_w].astype(jnp.float32)
+        total = keep[d, core, me_x, me_w]
         for step in range(1, wides):
             total = total + got_wide[d, step - 1].astype(jnp.float32)
         total = total.astype(jnp.bfloat16)
@@ -269,6 +271,7 @@
             pltpu.VMEM((count, planes * 6 * lanes), low),
             pltpu.VMEM((count, planes * 6 * lanes), low),
             pltpu.VMEM((2, count, count), jnp.float32),
+            pltpu.VMEM((3, 2, across, wides, share, count), jnp.float32),
             pltpu.VMEM((3, 2, across, wides, share, count), low),
             pltpu.VMEM((3, across, wides, share, count), low),
             pltpu.VMEM((3, across - 1, wides, share, count), low),

time: 57.5 us -> 57.4 us (level)
  no operation moved by 1% of the time
where the time goes in v3:
time: 57.4 us; the launch traced here: 57.3 us
  Pallas kernels  53.3 us (93%)
  local copies, waits for them, and re-layouts  3.29 us (6%)
  between operations  0.69 us (1%)
    pallas_call x1, Pallas kernels, on_device(): pl.pallas_call(functools.partial(kernel, wides, narrows, norm), out_shape...  53.3 us
    transpose x1, local copies, waits for them, and re-layouts, on_device(): turned = vectors.transpose(3, 1, 2, 0, 4).reshape(planes, 6, count, lanes)  1.72 us
    unnamed x8, local copies, waits for them, and re-layouts  1.57 us

profile of v3, /device:TPU:0, one launch (start us, length us, event | category | flops | bytes accessed | tf_op | source)
XLA Modules:
  0.0 57.3 jit_solution(1294423707271070481)
XLA Ops:
  0.6 0.0 copy-start
  0.6 0.0 copy-start.1
  0.7 0.0 copy-start.2
  0.7 1.7 %copy.6 = bf16[2,2,3,512,128]{4,3,2,1,0:T(8,128)(2,1)S(1)} copy(bf16[2,2,3,512,128]{4,0,2,1,3:T(2,128)(2,1)} %bitcast.3) | data formatting | bytes 3145728 | tf_op jit(solution)/shard_map/transpose | solution.py:255
  2.4 0.0 copy-done
  2.4 0.0 copy-done.1
  2.4 0.0 copy-done.2
  2.4 53.3 %shard_map.59 = (f32[3,2,64,512]{3,2,1,0:T(8,128)S(1)}, f32[3,2,64,64]{3,2,1,0:T(8,128)S(1)}) custom-call(bf16[2,6,512,128]{3,2,1,0:T(8,128)(2,1)S(1)} %bitcast.2, f32[3,2,3,3,2,128]{5,4,3,2,1,0:T(2,128)S(1)} %copy-done, s32[3]{0:T(128)S(1)} %copy-done.2, bf16[2,64,64]{2,1,0:T(8,128)(2,1)S(1)} %copy-done.1), custom_call_target="tpu_custom_call" | custom-call | tf_op jit(solution)/shard_map/pallas_call | solution.py:259
  55.7 0.9 %copy.9 = f32[3,2,64,512]{3,2,1,0:T(8,128)} copy(f32[3,2,64,512]{3,2,1,0:T(8,128)S(1)} %get-tuple-element.4) | data formatting | bytes 1572864
  56.6 0.7 %copy.10 = f32[3,2,64,64]{3,2,1,0:T(8,128)} copy(f32[3,2,64,64]{3,2,1,0:T(8,128)S(1)} %get-tuple-element.5) | data formatting | bytes 196608
Async XLA Ops:
  0.6 1.8 %copy-start = (f32[3,2,3,3,2,128]{5,4,3,2,1,0:T(2,128)S(1)}, f32[3,2,3,3,2,128]{5,4,3,2,1,0:T(2,128)}, u32[]{:S(2)}) copy-start(f32[3,2,3,3,2,128]{5,4,3,2,1,0:T(2,128)} %links.1) | copy-start | bytes 165892
  0.6 1.8 %copy-start.1 = (bf16[2,64,64]{2,1,0:T(8,128)(2,1)S(1)}, bf16[2,64,64]{2,1,0:T(8,128)(2,1)}, u32[]{:S(2)}) copy-start(bf16[2,64,64]{2,1,0:T(8,128)(2,1)} %peram.1) | copy-start | bytes 49156
  0.7 1.8 %copy-start.2 = (s32[3]{0:T(128)S(1)}, s32[3]{0:T(128)}, u32[]{:S(2)}) copy-start(s32[3]{0:T(128)} %dirs.1) | copy-start | bytes 40

commit v4 on v3

--- a/solution.py
+++ b/solution.py
@@ -67,13 +67,12 @@
         pack[plane, comp, pl.ds(start, CHUNK), :] = total.astype(jnp.bfloat16)
         return carry
 
-    lax.fori_loop(0, planes * comps * (per_group // CHUNK), pack_rows, 0)
-
     pl.semaphore_wait(barrier, wides + narrows - 2)
     first_copy = copy(vec.at[0], halo0, h_send.at[0], h_recv.at[0], at_wide(wides - 1))
     second_copy = copy(pack, halo1, h_send.at[1], h_recv.at[1], at_narrow(narrows - 1))
+    first_copy.start()
+    lax.fori_loop(0, planes * comps * (per_group // CHUNK), pack_rows, 0)
     second_copy.start()
-    first_copy.start()
     per_copies = [
         copy(peram, per_all.at[me_w], p_send.at[step - 1], p_recv.at[step - 1], at_wide(step))
         for step in range(1, wides)
@@ -98,8 +97,8 @@
         return jnp.where(
             lax.rem(lane, LZ) < LZ - 1, pltpu.roll(own, lanes - 1, 1), pltpu.roll(own, LZ - 1, 1))
 
-    def forward(direction):
-        for plane in range(planes):
+    def forward(direction, planes_here=None):
+        for plane in planes_here or range(planes):
             def chunk(i, carry):
                 start = pl.multiple_of(i * CHUNK, CHUNK)
                 values = [shifted(direction, plane, comp, start) for comp in range(comps)]
@@ -125,7 +124,6 @@
             lax.fori_loop(0, count // CHUNK, chunk, 0)
 
     def compute(direction):
-        forward(direction)
         left = jnp.concatenate(
             [vec[plane, comp] for plane in range(planes) for comp in range(comps)], 1)
         half[0] = lax.dot_general(left, f_re[...], NT, preferred_element_type=jnp.float32)
@@ -214,17 +212,21 @@
         prods[d, 0] = times(real, per_r) - times(imag, per_i)
         prods[d, 1] = times(real, per_i) + times(imag, per_r)
 
+    forward(2)
     compute(2)
     core_copy(2).start()
     second_copy.wait()
+    forward(1)
+    core_done(2)
     compute(1)
     core_copy(1).start()
-    core_done(2)
+    forward(0, range(planes - 1))
+    core_done(1)
+    row_done(2)
     first_copy.wait()
+    forward(0, range(planes - 1, planes))
     compute(0)
     core_copy(0).start()
-    row_done(2)
-    core_done(1)
     core_done(0)
     row_done(1)
     wide_done(2)

time: 57.4 us -> 54.7 us (0.953); the launches traced: 57.3 us -> 54 us
  Pallas kernels: 53.3 us -> 50 us
    pallas_call x1, Pallas kernels: 53.3 us -> 50 us  [on_device(): pl.pallas_call(functools.partial(kernel, wides, narrows, norm), out_shape...]
where the time goes in v4:
time: 54.7 us; the launch traced here: 54 us
  Pallas kernels  50 us (91%)
  local copies, waits for them, and re-layouts  3.29 us (6%)
  between operations  0.69 us (1%)
    pallas_call x1, Pallas kernels, on_device(): pl.pallas_call(functools.partial(kernel, wides, narrows, norm), out_shape...  50 us
    transpose x1, local copies, waits for them, and re-layouts, on_device(): turned = vectors.transpose(3, 1, 2, 0, 4).reshape(planes, 6, count, lanes)  1.72 us
    unnamed x8, local copies, waits for them, and re-layouts  1.57 us

profile of v4, /device:TPU:0, one launch (start us, length us, event | category | flops | bytes accessed | tf_op | source)
XLA Modules:
  0.0 54.0 jit_solution(16790955914829429765)
XLA Ops:
  0.6 0.0 copy-start
  0.6 0.0 copy-start.1
  0.7 0.0 copy-start.2
  0.7 1.7 %copy.6 = bf16[2,2,3,512,128]{4,3,2,1,0:T(8,128)(2,1)S(1)} copy(bf16[2,2,3,512,128]{4,0,2,1,3:T(2,128)(2,1)} %bitcast.3) | data formatting | bytes 3145728 | tf_op jit(solution)/shard_map/transpose | solution.py:257
  2.4 0.0 copy-done
  2.4 0.0 copy-done.1
  2.4 0.0 copy-done.2
  2.4 50.0 %shard_map.59 = (f32[3,2,64,512]{3,2,1,0:T(8,128)S(1)}, f32[3,2,64,64]{3,2,1,0:T(8,128)S(1)}) custom-call(bf16[2,6,512,128]{3,2,1,0:T(8,128)(2,1)S(1)} %bitcast.2, f32[3,2,3,3,2,128]{5,4,3,2,1,0:T(2,128)S(1)} %copy-done, s32[3]{0:T(128)S(1)} %copy-done.2, bf16[2,64,64]{2,1,0:T(8,128)(2,1)S(1)} %copy-done.1), custom_call_target="tpu_custom_call" | custom-call | tf_op jit(solution)/shard_map/pallas_call | solution.py:261
  52.4 0.9 %copy.9 = f32[3,2,64,512]{3,2,1,0:T(8,128)} copy(f32[3,2,64,512]{3,2,1,0:T(8,128)S(1)} %get-tuple-element.4) | data formatting | bytes 1572864
  53.3 0.7 %copy.10 = f32[3,2,64,64]{3,2,1,0:T(8,128)} copy(f32[3,2,64,64]{3,2,1,0:T(8,128)S(1)} %get-tuple-element.5) | data formatting | bytes 196608
Async XLA Ops:
  0.6 1.8 %copy-start = (f32[3,2,3,3,2,128]{5,4,3,2,1,0:T(2,128)S(1)}, f32[3,2,3,3,2,128]{5,4,3,2,1,0:T(2,128)}, u32[]{:S(2)}) copy-start(f32[3,2,3,3,2,128]{5,4,3,2,1,0:T(2,128)} %links.1) | copy-start | bytes 165892
  0.6 1.8 %copy-start.1 = (bf16[2,64,64]{2,1,0:T(8,128)(2,1)S(1)}, bf16[2,64,64]{2,1,0:T(8,128)(2,1)}, u32[]{:S(2)}) copy-start(bf16[2,64,64]{2,1,0:T(8,128)(2,1)} %peram.1) | copy-start | bytes 49156
  0.7 1.8 %copy-start.2 = (s32[3]{0:T(128)S(1)}, s32[3]{0:T(128)}, u32[]{:S(2)}) copy-start(s32[3]{0:T(128)} %dirs.1) | copy-start | bytes 40
